TPU v7x, 32 devices: a whole 2x2x4 slice. The times are simulated.
32 devices in a mesh: wide: 16 (over z, y, core), blk: 2 (over x).
Axes of the slice: x: 2, y: 2, z: 4, core: 2. Of those that a mesh axis runs over, the one named last changes fastest.
Arguments:
- position: float32 [3, 4096], P(None, ('wide', 'blk')), may hold values from -1 to 1, as said below
- order_field: float32 [12, 4096], P(None, ('wide', 'blk')), may hold values from -1.5 to 1.5
- cell_area: float32 [4096], P(('wide', 'blk')), may hold values from 0.5 to 2
- slot_vertex: int32 [16, 2, 16, 24], P('wide', 'blk'), may hold values from 0 to 127
- send_count: int32 [16, 2, 16], P('wide', 'blk'), may hold values from 0 to 24, as said below
- corner_slot: int32 [16, 2, 3, 256], P('wide', 'blk'), may hold values from 0 to 383, as said below
- edge_weight: float32 [16, 2, 3, 256], P('wide', 'blk'), may hold values from 0.2 to 2
Outputs:
- potential: float32 [12, 4096], P(None, ('wide', 'blk'))
Inputs may be any that keep to these rules, and one draw needn't show every extreme that they name: `position`: each column is a unit vector. `slot_vertex`: slots of a block at or beyond the matching send_count are padding and hold arbitrary numbers. send_count[p, b, q] is how many leading slots of block [p, b, q] are live. It is nonzero exactly when (q - p) mod 16 is one of 0, 1, 2, 8, 15, 14, and then at least 12; every owner keeps all 24 slots live for one of the five requesters with (q - p) mod 16 among 0, 1, 2, 15, 14. `corner_slot`: A value c of requester (q, b) names slot c % 24 of owner (c // 24, b); it is always a live slot, and every live slot is named by some corner.
All inputs are finite; a program needn't handle non-finite values.
Results may differ from a plain program's by a relative error of at most 0.0003.
Values sent between devices are 32-bit elements; how exact they have to be, the bound alone decides.
A program may use at most 64 MiB of HBM per device.

v0:
```python
import math
import jax
import jax.numpy as jnp
from jax import lax
from jax.sharding import PartitionSpec as P

stiff_coef = 0.1
source_block = 2048


def shifted(block, axis, distance):
    devices = range(lax.axis_size(axis))
    route = [((i - distance) % len(devices), i) for i in devices]
    return lax.ppermute(block, axis, route)


def kernel_sum(targets, sources, weights, soften):
    number = sources.shape[1]
    block_len = math.gcd(number, source_block)

    def add_block(block_id, running):
        first_col = block_id * block_len
        source_pos = lax.dynamic_slice_in_dim(sources, first_col, block_len, 1)
        source_mass = lax.dynamic_slice_in_dim(weights, first_col, block_len, 1)
        distance = (targets[0][:, None] - source_pos[0][None, :]) ** 2
        distance = distance + (targets[1][:, None] - source_pos[1][None, :]) ** 2
        distance = distance + (targets[2][:, None] - source_pos[2][None, :]) ** 2
        kernel = jnp.log(distance + soften)
        return running + jnp.einsum(
            "fs,ts->ft", source_mass, kernel, precision=lax.Precision.HIGHEST
        )

    start_sum = jnp.zeros((weights.shape[0], targets.shape[1]), jnp.float32)
    return lax.fori_loop(0, number // block_len, add_block, start_sum)


def corner_terms(values, weights):
    value_a, value_b, value_c = (values[..., 0, :], values[..., 1, :], values[..., 2, :])
    weight_a, weight_b, weight_c = (weights[..., 0, :], weights[..., 1, :], weights[..., 2, :])
    term_a = weight_c * (value_a - value_b) + weight_b * (value_a - value_c)
    term_b = weight_c * (value_b - value_a) + weight_a * (value_b - value_c)
    term_c = weight_b * (value_c - value_a) + weight_a * (value_c - value_b)
    return jnp.stack([term_a, term_b, term_c], axis=-2)


def gather_sources(position, masses):
    return lax.all_gather(jnp.concatenate([position, masses], axis=0), "wide", axis=1, tiled=True)


def per_device(position, order_field, cell_area, slot_vertex, send_count, corner_slot, edge_weight):
    fields = order_field.shape[0]
    local_count = order_field.shape[1]
    blk_size = lax.axis_size("blk")
    all_verts = local_count * lax.axis_size("wide") * blk_size
    soften = 4.0 / all_verts
    strength = all_verts ** (-0.5)
    weighted, area_total = lax.psum(
        (jnp.sum(cell_area[None, :] * order_field, axis=1), jnp.sum(cell_area)), ("wide", "blk")
    )
    average = weighted / area_total
    masses = cell_area[None, :] * (order_field - average[:, None])
    pooled = gather_sources(position, masses)
    half_count = local_count // 2
    empty_sum = jnp.zeros((fields, half_count), jnp.float32)

    def turn_pair(turn_id, state_pair):
        upper_half, lower_half = state_pair
        targets = jnp.concatenate([upper_half[:3], lower_half[:3]], axis=1)
        increment = kernel_sum(targets, pooled[:3], pooled[3:], soften)
        upper_half = jnp.concatenate(
            [upper_half[:3], upper_half[3:] + increment[:, :half_count]], axis=0
        )
        lower_half = jnp.concatenate(
            [lower_half[:3], lower_half[3:] + increment[:, half_count:]], axis=0
        )
        upper_half = shifted(upper_half, "blk", 1)
        lower_half = shifted(lower_half, "blk", -1)
        return (upper_half, lower_half)

    start_pair = (
        jnp.concatenate([position[:, :half_count], empty_sum], axis=0),
        jnp.concatenate([position[:, half_count:], empty_sum], axis=0),
    )
    upper_half, lower_half = lax.fori_loop(0, blk_size, turn_pair, start_pair)
    summed = jnp.concatenate([upper_half[3:], lower_half[3:]], axis=1)
    long_range = -strength * summed
    owners = slot_vertex.shape[2]
    slot_len = slot_vertex.shape[3]
    slot_table = slot_vertex.reshape(owners, slot_len)
    live_slot = lax.broadcasted_iota(jnp.int32, (owners, slot_len), 1) < send_count.reshape(
        owners, 1
    )
    safe_slot = jnp.where(live_slot, slot_table, 0)
    outgoing = jnp.where(live_slot[None], order_field[:, safe_slot], 0.0)
    received = lax.all_to_all(outgoing, "wide", split_axis=1, concat_axis=1, tiled=True)
    flat_values = received.reshape(fields, owners * slot_len)
    corners = corner_slot.reshape(3, -1)
    picked = flat_values[:, corners]
    corner_sum = corner_terms(picked, edge_weight.reshape(3, -1))
    returned = (
        jnp.zeros((fields, owners * slot_len), jnp.float32)
        .at[:, corners.reshape(-1)]
        .add(corner_sum.reshape(fields, -1))
        .reshape(fields, owners, slot_len)
    )
    incoming = lax.all_to_all(returned, "wide", split_axis=1, concat_axis=1, tiled=True)
    masked = jnp.where(live_slot[None], incoming, 0.0)
    stiffness = (
        jnp.zeros((fields, local_count), jnp.float32)
        .at[:, safe_slot.reshape(-1)]
        .add(masked.reshape(fields, -1))
    )
    return order_field**3 - order_field + stiff_coef * stiffness / cell_area[None, :] + long_range


def solution(mesh):
    placed = (
        P(None, ("wide", "blk")),
        P(None, ("wide", "blk")),
        P(("wide", "blk")),
        P("wide", "blk", None, None),
        P("wide", "blk", None),
        P("wide", "blk", None, None),
        P("wide", "blk", None, None),
    )
    return jax.shard_map(
        per_device, mesh=mesh, in_specs=placed, out_specs=P(None, ("wide", "blk")), check_vma=False
    )
```

profile of v0, /device:TPU:0, one launch (start us, length us, event | category | flops | bytes accessed | tf_op | source)
XLA Modules:
  0.0 108.7 jit_solution(8041242663535604738)
XLA Ops:
  0.0 0.7 copy-done.6
  0.7 0.8 compare_select_fusion
  1.6 0.6 copy-done
  2.3 1.1 %gather_fusion = f32[384,12]{1,0:T(8,128)S(1)} fusion(f32[12,128]{0,1:T(8,128)S(1)} %copy.57, s32[1024]{0:T(1024)S(1)} %pad_clamp_fusion.1), kind=kCustom, calls=%fused_computation | custom fusion | bytes 38400 | tf_op jit(solution)/shard_map/gather | solution.py:94
  3.6 0.7 reshape.288
  4.3 7.4 %all-to-all-start = ((f32[16,1,288]{2,1,0:T(1,128)}), f32[16,1,288]{2,1,0:T(1,128)S(1)}, u32[]{:S(2)}, u32[]{:S(2)}) async-start(f32[16,1,288]{2,1,0:T(1,128)} %reshape.288), calls=%async_computation | async-start | bytes 49152 | tf_op jit(solution)/shard_map/all_to_all | solution.py:95
  11.9 0.6 copy-done.3
  12.5 0.7 copy-done.5
  13.3 0.6 reduce_sum.19
  14.0 40.9 %all-reduce.2 = (f32[12]{0:T(128)S(1)}, f32[]{:T(128)}) all-reduce(f32[12]{0:T(128)S(1)} %multiply_reduce_fusion, f32[]{:T(128)} %reduce_sum.19), channel_id=1, replica_groups=mesh['wide'=16,'blk'=2] {'wide','blk'}, use_global_device_ids=true, to_apply=%region_3.0 | all-reduce | flops 13 | bytes 104 | tf_op jit(solution)/shard_map/psum | solution.py:57
  54.9 0.7 broadcast_divide_fusion
  55.8 21.7 %all_gather.3 = f32[15,2048]{1,0:T(8,128)S(1)} all-gather(f32[15,128]{1,0:T(8,128)S(1)} %pad_maximum_fusion.4), channel_id=1, replica_groups=mesh['wide'=16,'blk'=2] {'wide'}, dimensions={1}, use_global_device_ids=true | all-gather | bytes 130560 | tf_op jit(solution)/shard_map/all_gather | solution.py:47
  77.5 0.5 broadcast.158
  78.0 0.7 reduce.6
  79.0 1.6 %gather_fusion.1 = f32[768,12]{1,0:T(8,128)S(1)} fusion(f32[12,384]{0,1:T(8,128)S(1)} %bitcast.57, s32[1024]{0:T(1024)S(1)} %pad_clamp_fusion), kind=kCustom, calls=%fused_computation.1 | custom fusion | bytes 76800 | tf_op jit(solution)/shard_map/gather | solution.py:98
  81.0 6.1 %scatter_custom_fusion = f32[12,384]{0,1:T(8,128)S(1)} fusion(s32[768]{0:T(1024)S(1)} %fusion.25, f32[768,12]{1,0:T(8,128)S(1)} %copy.62, f32[]{:T(128)} %constant.12.clone.1), kind=kCustom, calls=%fused_computation.33 | custom fusion | flops 9216 | bytes 18436 | tf_op jit(solution)/shard_map/scatter-add | solution.py:103
  87.3 0.7 reshape.290
  88.0 3.5 %all-to-all-start.1 = ((f32[16,1,288]{2,1,0:T(1,128)}), f32[16,1,288]{2,1,0:T(1,128)S(1)}, u32[]{:S(2)}, u32[]{:S(2)}) async-start(f32[16,1,288]{2,1,0:T(1,128)} %reshape.290), calls=%async_computation.1 | async-start | bytes 49152 | tf_op jit(solution)/shard_map/all_to_all | solution.py:106
  91.5 12.6 %while.12 = (s32[]{:T(128)}, f32[15,64]{1,0:T(8,128)S(1)}, f32[15,64]{1,0:T(8,128)S(1)}, f32[15,2048]{1,0:T(8,128)S(1)}, s32[]{:T(128)}) while((s32[]{:T(128)}, f32[15,64]{1,0:T(8,128)S(1)}, f32[15,64]{1,0:T(8,128)S(1)}, f32[15,2048]{1,0:T(8,128)S(1)}, s32[]{:T(128)}) %tuple.37), condition=%wide.region_7.0_spmd, body=%wide.region_6.7_spmd.sunk | while | flops 40111872 | bytes 278157 | solution.py:84
  91.6 1.3 %convolution_bitcast_fusion.2 = f32[12,128]{1,0:T(8,128)S(1)} fusion(f32[2048]{0:T(1024)S(1)} %bitcast.65, f32[128]{0:T(128)S(1)} %get-tuple-element.112, f32[2048]{0:T(1024)S(1)} %bitcast.66, f32[128]{0:T(128)S(1)} %get-tuple-element.114, f32[2048]{0:T(1024)S(1)} %bitcast.64, f32[128]{0:T(128)S(1)} %get-tuple-element.116, ...), kind=kOutput, calls=%fused_computation.4.clone.1 | convolution fusion | flops 40108032 | bytes 155136 | tf_op jit(solution)/shard_map/while/body/eval_jaxpr/while/body/eval_jaxpr/fs,ts->ft/dot_general | solution.py:29
  93.1 0.6 collective-permute-start.1
  93.6 1.5 %collective-permute-start = (f32[15,64]{1,0:T(8,128)S(1)}, f32[15,64]{1,0:T(8,128)S(1)}, u32[]{:S(2)}, u32[]{:S(2)}) collective-permute-start(f32[15,64]{1,0:T(8,128)S(1)} %pad_maximum_fusion.9), channel_id=1, source_target_pairs={{1,0},{0,1},{3,2},{2,3},{5,4},{4,5},{7,6},{6,7},{9,8},{8,9},{11,10... | collective-permute-start | bytes 11528 | tf_op jit(solution)/shard_map/while/body/eval_jaxpr/ppermute | solution.py:14
  95.2 1.6 %collective-permute-done.1 = f32[15,64]{1,0:T(8,128)S(1)} collective-permute-done((f32[15,64]{1,0:T(8,128)S(1)}, f32[15,64]{1,0:T(8,128)S(1)}, u32[]{:S(2)}, u32[]{:S(2)}) %collective-permute-start.1) | collective-permute-done | bytes 3872 | tf_op jit(solution)/shard_map/while/body/eval_jaxpr/ppermute | solution.py:14
  96.8 0.5 collective-permute-done
  97.4 1.3 %convolution_bitcast_fusion.2 = f32[12,128]{1,0:T(8,128)S(1)} fusion(f32[2048]{0:T(1024)S(1)} %bitcast.65, f32[128]{0:T(128)S(1)} %get-tuple-element.112, f32[2048]{0:T(1024)S(1)} %bitcast.66, f32[128]{0:T(128)S(1)} %get-tuple-element.114, f32[2048]{0:T(1024)S(1)} %bitcast.64, f32[128]{0:T(128)S(1)} %get-tuple-element.116, ...), kind=kOutput, calls=%fused_computation.4.clone.1 | convolution fusion | flops 40108032 | bytes 155136 | tf_op jit(solution)/shard_map/while/body/eval_jaxpr/while/body/eval_jaxpr/fs,ts->ft/dot_general | solution.py:29
  98.8 1.6 %collective-permute-start.1 = (f32[15,64]{1,0:T(8,128)S(1)}, f32[15,64]{1,0:T(8,128)S(1)}, u32[]{:S(2)}, u32[]{:S(2)}) collective-permute-start(f32[15,64]{1,0:T(8,128)S(1)} %pad_maximum_fusion.10), channel_id=1, source_target_pairs={{1,0},{0,1},{3,2},{2,3},{5,4},{4,5},{7,6},{6,7},{9,8},{8,9},{11,10... | collective-permute-start | bytes 11528 | tf_op jit(solution)/shard_map/while/body/eval_jaxpr/ppermute | solution.py:14
  100.4 0.5 collective-permute-start
  100.9 1.6 %collective-permute-done.1 = f32[15,64]{1,0:T(8,128)S(1)} collective-permute-done((f32[15,64]{1,0:T(8,128)S(1)}, f32[15,64]{1,0:T(8,128)S(1)}, u32[]{:S(2)}, u32[]{:S(2)}) %collective-permute-start.1) | collective-permute-done | bytes 3872 | tf_op jit(solution)/shard_map/while/body/eval_jaxpr/ppermute | solution.py:14
  102.5 1.5 %collective-permute-done = f32[15,64]{1,0:T(8,128)S(1)} collective-permute-done((f32[15,64]{1,0:T(8,128)S(1)}, f32[15,64]{1,0:T(8,128)S(1)}, u32[]{:S(2)}, u32[]{:S(2)}) %collective-permute-start) | collective-permute-done | bytes 3872 | tf_op jit(solution)/shard_map/while/body/eval_jaxpr/ppermute | solution.py:14
  104.1 0.7 reduce.7
  105.2 2.7 %scatter_custom_fusion.1 = f32[12,128]{0,1:T(8,128)S(1)} fusion(s32[384]{0:T(512)S(1)} %fusion.27, f32[384,12]{1,0:T(8,128)S(1)} %copy.65, f32[]{:T(128)} %constant.12.clone.1), kind=kCustom, calls=%fused_computation.37 | custom fusion | flops 4608 | bytes 6148 | tf_op jit(solution)/shard_map/scatter-add | solution.py:111
  108.0 0.7 fusion.24
  (66 shorter events, 2.7 us)
Async XLA Ops:
  0.0 0.7 copy-start.6
  1.5 0.7 copy-start
  4.3 73.1 %all-to-all-start = ((f32[16,1,288]{2,1,0:T(1,128)}), f32[16,1,288]{2,1,0:T(1,128)S(1)}, u32[]{:S(2)}, u32[]{:S(2)}) async-start(f32[16,1,288]{2,1,0:T(1,128)} %reshape.288), calls=%async_computation | async-start | bytes 49152 | tf_op jit(solution)/shard_map/all_to_all | solution.py:95
  11.8 0.7 copy-start.3
  12.5 0.7 copy-start.4
  12.5 0.7 copy-start.5
  13.2 0.7 copy-start.1
  54.9 0.7 copy-start.2
  88.0 16.1 %all-to-all-start.1 = ((f32[16,1,288]{2,1,0:T(1,128)}), f32[16,1,288]{2,1,0:T(1,128)S(1)}, u32[]{:S(2)}, u32[]{:S(2)}) async-start(f32[16,1,288]{2,1,0:T(1,128)} %reshape.290), calls=%async_computation.1 | async-start | bytes 49152 | tf_op jit(solution)/shard_map/all_to_all | solution.py:106
  93.1 3.7 %collective-permute-start.1 = (f32[15,64]{1,0:T(8,128)S(1)}, f32[15,64]{1,0:T(8,128)S(1)}, u32[]{:S(2)}, u32[]{:S(2)}) collective-permute-start(f32[15,64]{1,0:T(8,128)S(1)} %pad_maximum_fusion.10), channel_id=1, source_target_pairs={{1,0},{0,1},{3,2},{2,3},{5,4},{4,5},{7,6},{6,7},{9,8},{8,9},{11,10... | collective-permute-start | bytes 11528 | tf_op jit(solution)/shard_map/while/body/eval_jaxpr/ppermute | solution.py:14
  93.6 3.7 %collective-permute-start = (f32[15,64]{1,0:T(8,128)S(1)}, f32[15,64]{1,0:T(8,128)S(1)}, u32[]{:S(2)}, u32[]{:S(2)}) collective-permute-start(f32[15,64]{1,0:T(8,128)S(1)} %pad_maximum_fusion.9), channel_id=1, source_target_pairs={{1,0},{0,1},{3,2},{2,3},{5,4},{4,5},{7,6},{6,7},{9,8},{8,9},{11,10... | collective-permute-start | bytes 11528 | tf_op jit(solution)/shard_map/while/body/eval_jaxpr/ppermute | solution.py:14
  98.8 3.7 %collective-permute-start.1 = (f32[15,64]{1,0:T(8,128)S(1)}, f32[15,64]{1,0:T(8,128)S(1)}, u32[]{:S(2)}, u32[]{:S(2)}) collective-permute-start(f32[15,64]{1,0:T(8,128)S(1)} %pad_maximum_fusion.10), channel_id=1, source_target_pairs={{1,0},{0,1},{3,2},{2,3},{5,4},{4,5},{7,6},{6,7},{9,8},{8,9},{11,10... | collective-permute-start | bytes 11528 | tf_op jit(solution)/shard_map/while/body/eval_jaxpr/ppermute | solution.py:14
  100.4 3.7 %collective-permute-start = (f32[15,64]{1,0:T(8,128)S(1)}, f32[15,64]{1,0:T(8,128)S(1)}, u32[]{:S(2)}, u32[]{:S(2)}) collective-permute-start(f32[15,64]{1,0:T(8,128)S(1)} %pad_maximum_fusion.9), channel_id=1, source_target_pairs={{1,0},{0,1},{3,2},{2,3},{5,4},{4,5},{7,6},{6,7},{9,8},{8,9},{11,10... | collective-permute-start | bytes 11528 | tf_op jit(solution)/shard_map/while/body/eval_jaxpr/ppermute | solution.py:14
where the time goes:
time: 109 us
  blocking collectives  62.6 us (57%)
  starting transfers between devices  15.1 us (14%)
  other arithmetic  13.7 us (13%)
  local copies, waits for them, and re-layouts  9.1 us (8%)
  waiting for transfers between devices  5.28 us (5%)
  matrix products  2.63 us (2%)
    psum x1, blocking collectives, per_device(): lax.psum((jnp.sum(cell_area[None, :] * order_field, axis=1), jnp.sum(cell...  40.9 us
    all_gather x1, blocking collectives, gather_sources(): lax.all_gather(jnp.concatenate([position, masses], axis=0), 'wide', axis=...  21.7 us
    all_to_all x1, starting transfers between devices, per_device(): lax.all_to_all(outgoing, 'wide', split_axis=1, concat_axis=1, tiled=True)  7.41 us
    scatter-add x1, other arithmetic, per_device(): returned = jnp.zeros((fields, owners * slot_len), jnp.float32).at[:, corn...  6.08 us
    ppermute x4, waiting for transfers between devices, shifted(): return lax.ppermute(block, axis, route)  5.27 us
    unnamed x21, local copies, waits for them, and re-layouts  4.29 us
    ppermute x4, starting transfers between devices, shifted(): return lax.ppermute(block, axis, route)  4.18 us
    all_to_all x1, starting transfers between devices, per_device(): lax.all_to_all(returned, 'wide', split_axis=1, concat_axis=1, tiled=True)  3.49 us
  transfers between devices with their start and end apart: 6, of which 4 were waited for; matrix products, arithmetic and copies ran while one was open for 4% of the time, Pallas kernels for 0%

commit v1 on v0

--- a/solution.py
+++ b/solution.py
@@ -55,7 +55,8 @@
     soften = 4.0 / all_verts
     strength = all_verts ** (-0.5)
     weighted, area_total = lax.psum(
-        (jnp.sum(cell_area[None, :] * order_field, axis=1), jnp.sum(cell_area)), ("wide", "blk")
+        lax.psum((jnp.sum(cell_area[None, :] * order_field, axis=1), jnp.sum(cell_area)), "blk"),
+        "wide",
     )
     average = weighted / area_total
     masses = cell_area[None, :] * (order_field - average[:, None])

time: 109 us -> 103 us (0.945)
  blocking collectives: 62.6 us -> 56.3 us
    psum x1, blocking collectives: 40.9 us -> 5.57 us  [per_device(): lax.psum((jnp.sum(cell_area[None, :] * order_field, axis=1), jnp.sum(cell...]
    psum x0 -> x1, blocking collectives: none -> 33.3 us  [per_device(): lax.psum(lax.psum((jnp.sum(cell_area[None, :] * order_field, axis=1), jnp...]
    all_gather x1, blocking collectives: 21.7 us -> 17.5 us  [gather_sources(): lax.all_gather(jnp.concatenate([position, masses], axis=0), 'wide', axis=...]
  transfers between devices with their start and end apart: 6 -> 6, of which waited for: 4 -> 4; matrix products, arithmetic and copies ran while one was open for 4% -> 5% of each run, Pallas kernels for 0% -> 0%
where the time goes in v1:
time: 103 us; the launch traced here: 102 us
  blocking collectives  56.3 us (55%)
  starting transfers between devices  15.1 us (15%)
  other arithmetic  13.7 us (13%)
  local copies, waits for them, and re-layouts  9.1 us (9%)
  waiting for transfers between devices  5.28 us (5%)
  matrix products  2.63 us (3%)
    psum x1, blocking collectives, per_device(): lax.psum(lax.psum((jnp.sum(cell_area[None, :] * order_field, axis=1), jnp...  33.3 us
    all_gather x1, blocking collectives, gather_sources(): lax.all_gather(jnp.concatenate([position, masses], axis=0), 'wide', axis=...  17.5 us
    all_to_all x1, starting transfers between devices, per_device(): lax.all_to_all(outgoing, 'wide', split_axis=1, concat_axis=1, tiled=True)  7.41 us
    scatter-add x1, other arithmetic, per_device(): returned = jnp.zeros((fields, owners * slot_len), jnp.float32).at[:, corn...  6.08 us
    psum x1, blocking collectives, per_device(): lax.psum((jnp.sum(cell_area[None, :] * order_field, axis=1), jnp.sum(cell...  5.57 us
    ppermute x4, waiting for transfers between devices, shifted(): return lax.ppermute(block, axis, route)  5.27 us
    unnamed x21, local copies, waits for them, and re-layouts  4.29 us
    ppermute x4, starting transfers between devices, shifted(): return lax.ppermute(block, axis, route)  4.18 us
  transfers between devices with their start and end apart: 6, of which 4 were waited for; matrix products, arithmetic and copies ran while one was open for 5% of the time, Pallas kernels for 0%

profile of v1, /device:TPU:0, one launch (start us, length us, event | category | flops | bytes accessed | tf_op | source)
XLA Modules:
  0.0 102.5 jit_solution(6009111925804105729)
XLA Ops:
  0.0 0.7 copy-done.6
  0.7 0.8 compare_select_fusion
  1.6 0.6 copy-done
  2.3 1.1 %gather_fusion = f32[384,12]{1,0:T(8,128)S(1)} fusion(f32[12,128]{0,1:T(8,128)S(1)} %copy.57, s32[1024]{0:T(1024)S(1)} %pad_clamp_fusion.1), kind=kCustom, calls=%fused_computation | custom fusion | bytes 38400 | tf_op jit(solution)/shard_map/gather | solution.py:95
  3.6 0.7 reshape.288
  4.3 7.4 %all-to-all-start = ((f32[16,1,288]{2,1,0:T(1,128)}), f32[16,1,288]{2,1,0:T(1,128)S(1)}, u32[]{:S(2)}, u32[]{:S(2)}) async-start(f32[16,1,288]{2,1,0:T(1,128)} %reshape.288), calls=%async_computation | async-start | bytes 49152 | tf_op jit(solution)/shard_map/all_to_all | solution.py:96
  11.9 0.6 copy-done.3
  12.5 0.7 copy-done.5
  13.3 0.6 reduce_sum.19
  14.0 5.6 %all-reduce.3 = (f32[12]{0:T(128)S(1)}, f32[]{:T(128)}) all-reduce(f32[12]{0:T(128)S(1)} %multiply_reduce_fusion, f32[]{:T(128)} %reduce_sum.19), channel_id=1, replica_groups=mesh['wide'=16,'blk'=2] {'blk'}, use_global_device_ids=true, to_apply=%region_3.0 | all-reduce | flops 13 | bytes 104 | tf_op jit(solution)/shard_map/psum | solution.py:58
  19.6 33.3 %all-reduce.2 = (f32[12]{0:T(128)S(1)}, f32[]{:T(128)}) all-reduce(f32[12]{0:T(128)S(1)} %get-tuple-element.62, f32[]{:T(128)} %get-tuple-element.63), channel_id=1, replica_groups=mesh['wide'=16,'blk'=2] {'wide'}, use_global_device_ids=true, to_apply=%region_4.0 | all-reduce | flops 13 | bytes 104 | tf_op jit(solution)/shard_map/psum | solution.py:57
  52.9 0.7 broadcast_divide_fusion
  53.8 17.5 %all_gather.3 = f32[15,2048]{1,0:T(8,128)S(1)} all-gather(f32[15,128]{1,0:T(8,128)S(1)} %pad_maximum_fusion.4), channel_id=1, replica_groups=mesh['wide'=16,'blk'=2] {'wide'}, dimensions={1}, use_global_device_ids=true | all-gather | bytes 130560 | tf_op jit(solution)/shard_map/all_gather | solution.py:47
  71.3 0.5 broadcast.158
  71.8 0.7 reduce.6
  72.8 1.6 %gather_fusion.1 = f32[768,12]{1,0:T(8,128)S(1)} fusion(f32[12,384]{0,1:T(8,128)S(1)} %bitcast.57, s32[1024]{0:T(1024)S(1)} %pad_clamp_fusion), kind=kCustom, calls=%fused_computation.1 | custom fusion | bytes 76800 | tf_op jit(solution)/shard_map/gather | solution.py:99
  74.8 6.1 %scatter_custom_fusion = f32[12,384]{0,1:T(8,128)S(1)} fusion(s32[768]{0:T(1024)S(1)} %fusion.25, f32[768,12]{1,0:T(8,128)S(1)} %copy.62, f32[]{:T(128)} %constant.12.clone.1), kind=kCustom, calls=%fused_computation.33 | custom fusion | flops 9216 | bytes 18436 | tf_op jit(solution)/shard_map/scatter-add | solution.py:104
  81.0 0.7 reshape.290
  81.8 3.5 %all-to-all-start.1 = ((f32[16,1,288]{2,1,0:T(1,128)}), f32[16,1,288]{2,1,0:T(1,128)S(1)}, u32[]{:S(2)}, u32[]{:S(2)}) async-start(f32[16,1,288]{2,1,0:T(1,128)} %reshape.290), calls=%async_computation.1 | async-start | bytes 49152 | tf_op jit(solution)/shard_map/all_to_all | solution.py:107
  85.3 12.6 %while.12 = (s32[]{:T(128)}, f32[15,64]{1,0:T(8,128)S(1)}, f32[15,64]{1,0:T(8,128)S(1)}, f32[15,2048]{1,0:T(8,128)S(1)}, s32[]{:T(128)}) while((s32[]{:T(128)}, f32[15,64]{1,0:T(8,128)S(1)}, f32[15,64]{1,0:T(8,128)S(1)}, f32[15,2048]{1,0:T(8,128)S(1)}, s32[]{:T(128)}) %tuple.37), condition=%wide.region_9.0_spmd, body=%wide.region_8.9_spmd.sunk | while | flops 40111872 | bytes 278157 | solution.py:85
  85.4 1.3 %convolution_bitcast_fusion.2 = f32[12,128]{1,0:T(8,128)S(1)} fusion(f32[2048]{0:T(1024)S(1)} %bitcast.65, f32[128]{0:T(128)S(1)} %get-tuple-element.114, f32[2048]{0:T(1024)S(1)} %bitcast.66, f32[128]{0:T(128)S(1)} %get-tuple-element.116, f32[2048]{0:T(1024)S(1)} %bitcast.64, f32[128]{0:T(128)S(1)} %get-tuple-element.118, ...), kind=kOutput, calls=%fused_computation.4.clone.1 | convolution fusion | flops 40108032 | bytes 155136 | tf_op jit(solution)/shard_map/while/body/eval_jaxpr/while/body/eval_jaxpr/fs,ts->ft/dot_general | solution.py:29
  86.8 1.6 %collective-permute-start.1 = (f32[15,64]{1,0:T(8,128)S(1)}, f32[15,64]{1,0:T(8,128)S(1)}, u32[]{:S(2)}, u32[]{:S(2)}) collective-permute-start(f32[15,64]{1,0:T(8,128)S(1)} %pad_maximum_fusion.10), channel_id=1, source_target_pairs={{1,0},{0,1},{3,2},{2,3},{5,4},{4,5},{7,6},{6,7},{9,8},{8,9},{11,10... | collective-permute-start | bytes 11528 | tf_op jit(solution)/shard_map/while/body/eval_jaxpr/ppermute | solution.py:14
  88.9 1.6 %collective-permute-done.1 = f32[15,64]{1,0:T(8,128)S(1)} collective-permute-done((f32[15,64]{1,0:T(8,128)S(1)}, f32[15,64]{1,0:T(8,128)S(1)}, u32[]{:S(2)}, u32[]{:S(2)}) %collective-permute-start.1) | collective-permute-done | bytes 3872 | tf_op jit(solution)/shard_map/while/body/eval_jaxpr/ppermute | solution.py:14
  90.6 1.5 %collective-permute-done = f32[15,64]{1,0:T(8,128)S(1)} collective-permute-done((f32[15,64]{1,0:T(8,128)S(1)}, f32[15,64]{1,0:T(8,128)S(1)}, u32[]{:S(2)}, u32[]{:S(2)}) %collective-permute-start) | collective-permute-done | bytes 3872 | tf_op jit(solution)/shard_map/while/body/eval_jaxpr/ppermute | solution.py:14
  92.2 1.3 %convolution_bitcast_fusion.2 = f32[12,128]{1,0:T(8,128)S(1)} fusion(f32[2048]{0:T(1024)S(1)} %bitcast.65, f32[128]{0:T(128)S(1)} %get-tuple-element.114, f32[2048]{0:T(1024)S(1)} %bitcast.66, f32[128]{0:T(128)S(1)} %get-tuple-element.116, f32[2048]{0:T(1024)S(1)} %bitcast.64, f32[128]{0:T(128)S(1)} %get-tuple-element.118, ...), kind=kOutput, calls=%fused_computation.4.clone.1 | convolution fusion | flops 40108032 | bytes 155136 | tf_op jit(solution)/shard_map/while/body/eval_jaxpr/while/body/eval_jaxpr/fs,ts->ft/dot_general | solution.py:29
  93.6 0.6 collective-permute-start.1
  94.2 1.5 %collective-permute-start = (f32[15,64]{1,0:T(8,128)S(1)}, f32[15,64]{1,0:T(8,128)S(1)}, u32[]{:S(2)}, u32[]{:S(2)}) collective-permute-start(f32[15,64]{1,0:T(8,128)S(1)} %pad_maximum_fusion.9), channel_id=1, source_target_pairs={{1,0},{0,1},{3,2},{2,3},{5,4},{4,5},{7,6},{6,7},{9,8},{8,9},{11,10... | collective-permute-start | bytes 11528 | tf_op jit(solution)/shard_map/while/body/eval_jaxpr/ppermute | solution.py:14
  95.7 1.6 %collective-permute-done.1 = f32[15,64]{1,0:T(8,128)S(1)} collective-permute-done((f32[15,64]{1,0:T(8,128)S(1)}, f32[15,64]{1,0:T(8,128)S(1)}, u32[]{:S(2)}, u32[]{:S(2)}) %collective-permute-start.1) | collective-permute-done | bytes 3872 | tf_op jit(solution)/shard_map/while/body/eval_jaxpr/ppermute | solution.py:14
  97.3 0.5 collective-permute-done
  97.9 0.7 reduce.7
  99.0 2.7 %scatter_custom_fusion.1 = f32[12,128]{0,1:T(8,128)S(1)} fusion(s32[384]{0:T(512)S(1)} %fusion.27, f32[384,12]{1,0:T(8,128)S(1)} %copy.65, f32[]{:T(128)} %constant.12.clone.1), kind=kCustom, calls=%fused_computation.37 | custom fusion | flops 4608 | bytes 6148 | tf_op jit(solution)/shard_map/scatter-add | solution.py:112
  101.8 0.7 fusion.24
  (67 shorter events, 3.2 us)
Async XLA Ops:
  0.0 0.7 copy-start.6
  1.5 0.7 copy-start
  4.3 66.9 %all-to-all-start = ((f32[16,1,288]{2,1,0:T(1,128)}), f32[16,1,288]{2,1,0:T(1,128)S(1)}, u32[]{:S(2)}, u32[]{:S(2)}) async-start(f32[16,1,288]{2,1,0:T(1,128)} %reshape.288), calls=%async_computation | async-start | bytes 49152 | tf_op jit(solution)/shard_map/all_to_all | solution.py:96
  11.8 0.7 copy-start.3
  12.5 0.7 copy-start.4
  12.5 0.7 copy-start.5
  13.2 0.7 copy-start.1
  52.9 0.7 copy-start.2
  81.8 16.1 %all-to-all-start.1 = ((f32[16,1,288]{2,1,0:T(1,128)}), f32[16,1,288]{2,1,0:T(1,128)S(1)}, u32[]{:S(2)}, u32[]{:S(2)}) async-start(f32[16,1,288]{2,1,0:T(1,128)} %reshape.290), calls=%async_computation.1 | async-start | bytes 49152 | tf_op jit(solution)/shard_map/all_to_all | solution.py:107
  86.8 3.7 %collective-permute-start.1 = (f32[15,64]{1,0:T(8,128)S(1)}, f32[15,64]{1,0:T(8,128)S(1)}, u32[]{:S(2)}, u32[]{:S(2)}) collective-permute-start(f32[15,64]{1,0:T(8,128)S(1)} %pad_maximum_fusion.10), channel_id=1, source_target_pairs={{1,0},{0,1},{3,2},{2,3},{5,4},{4,5},{7,6},{6,7},{9,8},{8,9},{11,10... | collective-permute-start | bytes 11528 | tf_op jit(solution)/shard_map/while/body/eval_jaxpr/ppermute | solution.py:14
  88.4 3.7 %collective-permute-start = (f32[15,64]{1,0:T(8,128)S(1)}, f32[15,64]{1,0:T(8,128)S(1)}, u32[]{:S(2)}, u32[]{:S(2)}) collective-permute-start(f32[15,64]{1,0:T(8,128)S(1)} %pad_maximum_fusion.9), channel_id=1, source_target_pairs={{1,0},{0,1},{3,2},{2,3},{5,4},{4,5},{7,6},{6,7},{9,8},{8,9},{11,10... | collective-permute-start | bytes 11528 | tf_op jit(solution)/shard_map/while/body/eval_jaxpr/ppermute | solution.py:14
  93.6 3.7 %collective-permute-start.1 = (f32[15,64]{1,0:T(8,128)S(1)}, f32[15,64]{1,0:T(8,128)S(1)}, u32[]{:S(2)}, u32[]{:S(2)}) collective-permute-start(f32[15,64]{1,0:T(8,128)S(1)} %pad_maximum_fusion.10), channel_id=1, source_target_pairs={{1,0},{0,1},{3,2},{2,3},{5,4},{4,5},{7,6},{6,7},{9,8},{8,9},{11,10... | collective-permute-start | bytes 11528 | tf_op jit(solution)/shard_map/while/body/eval_jaxpr/ppermute | solution.py:14
  94.2 3.7 %collective-permute-start = (f32[15,64]{1,0:T(8,128)S(1)}, f32[15,64]{1,0:T(8,128)S(1)}, u32[]{:S(2)}, u32[]{:S(2)}) collective-permute-start(f32[15,64]{1,0:T(8,128)S(1)} %pad_maximum_fusion.9), channel_id=1, source_target_pairs={{1,0},{0,1},{3,2},{2,3},{5,4},{4,5},{7,6},{6,7},{9,8},{8,9},{11,10... | collective-permute-start | bytes 11528 | tf_op jit(solution)/shard_map/while/body/eval_jaxpr/ppermute | solution.py:14
